TPU v7x, 32 devices: a whole 2x2x4 slice. The times are simulated.
32 devices in a mesh: dp: 8 (over y, x, core), mp: 4 (over z).
Axes of the slice: x: 2, y: 2, z: 4, core: 2. Of those that a mesh axis runs over, the one named last changes fastest.
Arguments:
- tokens: bfloat16 [11264, 768], P('dp'), may hold values from -6 to 6
- lang: int32 [16], P('dp'), may hold values from 0 to 7
- page_len: int32 [16], P('dp'), may hold values from 374 to 561, as said below
- rel_pos: int32 [16, 704, 704], P('dp', 'mp'), may hold values from 0 to 31, as said below
- rel_x: int32 [16, 704, 704], P('dp', 'mp'), may hold values from 0 to 63, as said below
- rel_y: int32 [16, 704, 704], P('dp', 'mp'), may hold values from 0 to 63, as said below
- lang_table: float32 [8, 768], replicated, may hold values from -3 to 3
- convolution_weight: float32 [3, 768], replicated, may hold values from -2.4 to 2.4
- conv_b: float32 [768], replicated, may hold values from -1.8 to 1.8
- w_qkv: bfloat16 [768, 3, 768], P(None, None, 'mp'), may hold values from -0.21875 to 0.21875
- b_qv: float32 [2, 768], P(None, 'mp'), may hold values from -1.8 to 1.8
- bias_table: float32 [160, 12], replicated, may hold values from -3 to 3
- w_out: bfloat16 [768, 768], P('mp'), may hold values from -1.5 to 1.5
- b_out: float32 [768], replicated, may hold values from -1.8 to 1.8
- ln1_gain: float32 [768], replicated, may hold values from 0.5 to 1.5
- ln1_bias: float32 [768], replicated, may hold values from -1.8 to 1.8
- w_in: bfloat16 [768, 3072], P(None, 'mp'), may hold values from -0.21875 to 0.21875
- b_in: float32 [3072], P('mp'), may hold values from -1.8 to 1.8
- w_down: bfloat16 [3072, 768], P('mp'), may hold values from -0.109375 to 0.109375
- b_down: float32 [768], replicated, may hold values from -1.8 to 1.8
- ln2_gain: float32 [768], replicated, may hold values from 0.5 to 1.5
- ln2_bias: float32 [768], replicated, may hold values from -1.8 to 1.8
- cotangent: bfloat16 [11264, 768], P('dp'), may hold values from -6 to 6
Outputs:
- out: bfloat16 [11264, 768], P('dp')
- d_tokens: bfloat16 [11264, 768], P('dp')
- d_lang_table: float32 [8, 768], replicated
- d_conv_w: float32 [3, 768], replicated
- d_conv_b: float32 [768], replicated
- d_w_qkv: float32 [768, 3, 768], P(None, None, 'mp')
- d_b_qv: float32 [2, 768], P(None, 'mp')
- d_bias_table: float32 [160, 12], replicated
- d_w_out: float32 [768, 768], P('mp')
- d_b_out: float32 [768], replicated
- d_ln1_gain: float32 [768], replicated
- d_ln1_bias: float32 [768], replicated
- d_w_in: float32 [768, 3072], P(None, 'mp')
- d_b_in: float32 [3072], P('mp')
- d_w_down: float32 [3072, 768], P('mp')
- d_b_down: float32 [768], replicated
- d_ln2_gain: float32 [768], replicated
- d_ln2_bias: float32 [768], replicated
Inputs may be any that keep to these rules, and one draw needn't show every extreme that they name: `page_len`: the live tokens of a page fill its first slots; one page has exactly 561. `rel_pos`: bucket of the key's reading position minus the query's; positive offsets take the upper 32 // 2 buckets. `rel_x`: bucket of the key's horizontal coordinate minus the query's; positive offsets take the upper 64 // 2 buckets. `rel_y`: bucket of the key's vertical coordinate minus the query's; positive offsets take the upper 64 // 2 buckets.
All inputs are finite; a program needn't handle non-finite values.
Results may differ from a plain program's by a relative error of at most 0.02.
The roundings to bfloat16 on the way count: a program that leaves them out, or rounds other values in their place, can miss the bound.
Values may be sent and summed in bfloat16 or wider, within the bound.
No kernel may reach another device: no remote copies, remote signals or barrier semaphores. Data moves between devices by JAX's collectives and lax.ppermute only.
A program may use at most 256 MiB of HBM per device.

v0:
```python
import math
import jax
import jax.numpy as jnp
from jax import lax
from jax.sharding import PartitionSpec as P

HD = 64
NB1 = 32
NB2 = 64
CONV_TAPS = 3
CONV_DILATION = 2
norm_eps = 1e-05
masked_score = -1000000000.0


def layer_norm(inputs, norm_gain, norm_shift):
    row_mean = jnp.mean(inputs, axis=-1, keepdims=True)
    centred = inputs - row_mean
    spread = jnp.mean(centred * centred, axis=-1, keepdims=True)
    return centred * lax.rsqrt(spread + norm_eps) * norm_gain + norm_shift


def exact_gelu(inputs):
    return jax.nn.gelu(inputs, approximate=False)


def contract_rows(left_side, right_side):
    return lax.dot_general(
        left_side, right_side, (((0,), (0,)), ((), ())), preferred_element_type=jnp.float32
    )


def contract_cols(left_side, right_side):
    return lax.dot_general(
        left_side, right_side, (((1,), (1,)), ((), ())), preferred_element_type=jnp.float32
    )


def bucket_hits(pos_ids, x_ids, y_ids):
    bucket_index = lax.broadcasted_iota(jnp.int32, (NB1 + 2 * NB2, 1), 0)
    first_hit = bucket_index == pos_ids.reshape(1, -1)
    second = bucket_index == x_ids.reshape(1, -1) + NB1
    third_hit = bucket_index == y_ids.reshape(1, -1) + NB1 + NB2
    return first_hit | second | third_hit


def id_blocks(id_array, block_rows):
    page_count, row_count, col_count = id_array.shape
    return id_array.reshape(page_count * row_count // block_rows, block_rows, col_count)


def table_bias(table_rows, pos_ids, x_ids, y_ids):
    page_count, row_count, col_count = pos_ids.shape
    block_rows = math.gcd(row_count, 64)
    head_count = table_rows.shape[0]

    def one_block(pieces):
        bucket_hit = bucket_hits(pieces[0], pieces[1], pieces[2]).astype(jnp.float32)
        looked_up = jnp.dot(table_rows, bucket_hit, precision=lax.Precision.HIGHEST)
        return looked_up.astype(jnp.bfloat16).reshape(head_count, block_rows, col_count)

    blocks = lax.map(
        one_block,
        (
            id_blocks(pos_ids, block_rows),
            id_blocks(x_ids, block_rows),
            id_blocks(y_ids, block_rows),
        ),
    )
    blocks = blocks.reshape(page_count, row_count // block_rows, head_count, block_rows, col_count)
    return jnp.transpose(blocks, (0, 2, 1, 3, 4)).reshape(
        page_count, head_count, row_count, col_count
    )


def table_grad(score_grad, pos_ids, x_ids, y_ids):
    page_count, head_count, row_count, col_count = score_grad.shape
    block_rows = math.gcd(row_count, 64)
    block_count = page_count * row_count // block_rows
    grad_blocks = score_grad.reshape(
        page_count, head_count, row_count // block_rows, block_rows * col_count
    )
    grad_blocks = jnp.transpose(grad_blocks, (0, 2, 1, 3)).reshape(
        block_count, head_count, block_rows * col_count
    )

    def add_block(running, pieces):
        bucket_hit = bucket_hits(pieces[1], pieces[2], pieces[3]).astype(jnp.bfloat16)
        return (running + contract_cols(pieces[0], bucket_hit), None)

    zero_start = jnp.zeros((head_count, NB1 + 2 * NB2), jnp.float32)
    running, unused = lax.scan(
        add_block,
        zero_start,
        (
            grad_blocks,
            id_blocks(pos_ids, block_rows),
            id_blocks(x_ids, block_rows),
            id_blocks(y_ids, block_rows),
        ),
    )
    return running


def body(
    tokens,
    lang,
    page_len,
    rel_pos,
    rel_x,
    rel_y,
    lang_table,
    convolution_weight,
    conv_b,
    w_qkv,
    b_qv,
    bias_table,
    w_out,
    b_out,
    ln1_gain,
    ln1_bias,
    w_in,
    b_in,
    w_down,
    b_down,
    ln2_gain,
    ln2_bias,
    cotangent,
):
    page_count = page_len.shape[0]
    count_of_slots = rel_pos.shape[2]
    model_width = tokens.shape[1]
    local_cols = w_qkv.shape[2]
    heads_here = local_cols // HD
    total_rows = page_count * count_of_slots
    score_scale = HD ** (-0.5)
    slot_index = lax.broadcasted_iota(jnp.int32, (page_count, count_of_slots), 1)
    live_mask = slot_index < page_len[:, None]
    live_rows = live_mask.astype(jnp.float32)[:, :, None]
    key_live = live_mask[:, None, None, :]
    languages = lax.broadcasted_iota(jnp.int32, (1, lang_table.shape[0]), 1)
    lang_pick = (lang[:, None] == languages).astype(jnp.float32)
    convolution_reach = CONV_TAPS // 2 * CONV_DILATION

    def embed(tok_in, lang_weights, kernel_taps, kernel_bias):
        with_lang = (
            tok_in + jnp.dot(lang_pick, lang_weights, precision=lax.Precision.HIGHEST)[:, None, :]
        )
        padded_rows = jnp.pad(
            with_lang * live_rows, ((0, 0), (convolution_reach, convolution_reach), (0, 0))
        )
        convolution_sum = kernel_bias
        for index_of_tap in range(CONV_TAPS):
            convolution_sum = (
                convolution_sum
                + kernel_taps[index_of_tap]
                * padded_rows[
                    :, index_of_tap * CONV_DILATION : index_of_tap * CONV_DILATION + count_of_slots
                ]
            )
        return with_lang + convolution_sum

    tok_in = tokens.astype(jnp.float32).reshape(page_count, count_of_slots, model_width)
    first_pages, embed_back = jax.vjp(embed, tok_in, lang_table, convolution_weight, conv_b)
    first_in = first_pages.reshape(total_rows, model_width)
    first_low = first_in.astype(jnp.bfloat16)
    qkv_flat = w_qkv.reshape(model_width, 3 * local_cols)
    projected = jnp.dot(first_low, qkv_flat, preferred_element_type=jnp.float32).reshape(
        total_rows, 3, local_cols
    )
    head_shape = (page_count, count_of_slots, heads_here, HD)
    queries = (projected[:, 0] + b_qv[0]).astype(jnp.bfloat16).reshape(head_shape)
    key_rows = projected[:, 1].astype(jnp.bfloat16).reshape(head_shape)
    value_rows = (projected[:, 2] + b_qv[1]).astype(jnp.bfloat16).reshape(head_shape)
    row_bias = table_bias(jnp.transpose(bias_table), rel_pos, rel_x, rel_y)
    head_bias = lax.all_to_all(row_bias, "mp", split_axis=1, concat_axis=2, tiled=True)
    scores = (
        jnp.einsum("pqhd,pkhd->phqk", queries, key_rows, preferred_element_type=jnp.float32)
        * score_scale
    )
    scores = jnp.where(key_live, scores + head_bias.astype(jnp.float32), masked_score)
    top_score = jnp.max(scores, axis=-1, keepdims=True)
    exp_scores = jnp.exp(scores - top_score)
    probs_full = exp_scores / jnp.sum(exp_scores, axis=-1, keepdims=True)
    probs_low = probs_full.astype(jnp.bfloat16)
    mixed_heads = jnp.einsum(
        "phqk,pkhd->pqhd", probs_low, value_rows, preferred_element_type=jnp.float32
    )
    mixed_low = mixed_heads.astype(jnp.bfloat16).reshape(total_rows, local_cols)
    attn_part = jnp.dot(mixed_low, w_out, preferred_element_type=jnp.float32)
    attn_sum = lax.psum(attn_part.astype(jnp.bfloat16), "mp").astype(jnp.float32)
    resid_one = first_in + attn_sum + b_out
    hidden_one, norm_one_back = jax.vjp(layer_norm, resid_one, ln1_gain, ln1_bias)
    hidden_low = hidden_one.astype(jnp.bfloat16)
    pre_act = jnp.dot(hidden_low, w_in, preferred_element_type=jnp.float32) + b_in
    activation, gelu_back = jax.vjp(exact_gelu, pre_act)
    activ_low = activation.astype(jnp.bfloat16)
    ffn_part = jnp.dot(activ_low, w_down, preferred_element_type=jnp.float32)
    ffn_sum = lax.psum(ffn_part.astype(jnp.bfloat16), "mp").astype(jnp.float32)
    resid_two = hidden_one + ffn_sum + b_down
    result, norm_two_back = jax.vjp(layer_norm, resid_two, ln2_gain, ln2_bias)
    grad_two, d_ln2_gain, d_ln2_bias = norm_two_back(cotangent.astype(jnp.float32))
    d_b_down = jnp.sum(grad_two, axis=0)
    grad_ffn = grad_two.astype(jnp.bfloat16)
    d_w_down = contract_rows(activ_low, grad_ffn)
    grad_act = contract_cols(grad_ffn, w_down)
    grad_pre = gelu_back(grad_act)[0].astype(jnp.bfloat16)
    d_w_in = contract_rows(hidden_low, grad_pre)
    d_b_in = jnp.sum(grad_pre.astype(jnp.float32), axis=0)
    ffn_back = contract_cols(grad_pre, w_in)
    grad_hidden = grad_two + lax.psum(ffn_back.astype(jnp.bfloat16), "mp").astype(jnp.float32)
    grad_one, d_ln1_gain, d_ln1_bias = norm_one_back(grad_hidden)
    d_b_out = jnp.sum(grad_one, axis=0)
    grad_attn = grad_one.astype(jnp.bfloat16)
    d_w_out = contract_rows(mixed_low, grad_attn)
    grad_mixed = contract_cols(grad_attn, w_out).astype(jnp.bfloat16).reshape(head_shape)
    d_values = jnp.einsum(
        "phqk,pqhd->pkhd", probs_low, grad_mixed, preferred_element_type=jnp.float32
    ).astype(jnp.bfloat16)
    grad_probs = jnp.einsum(
        "pqhd,pkhd->phqk", grad_mixed, value_rows, preferred_element_type=jnp.float32
    )
    grad_scores = probs_full * (
        grad_probs - jnp.sum(probs_full * grad_probs, axis=-1, keepdims=True)
    )
    grad_scores = grad_scores.astype(jnp.bfloat16)
    d_queries = (
        jnp.einsum("phqk,pkhd->pqhd", grad_scores, key_rows, preferred_element_type=jnp.float32)
        * score_scale
    ).astype(jnp.bfloat16)
    d_keys = (
        jnp.einsum("phqk,pqhd->pkhd", grad_scores, queries, preferred_element_type=jnp.float32)
        * score_scale
    ).astype(jnp.bfloat16)
    grad_qkv = jnp.stack([d_queries, d_keys, d_values], axis=2).reshape(total_rows, 3 * local_cols)
    d_w_qkv = contract_rows(first_low, grad_qkv).reshape(model_width, 3, local_cols)
    grad_cols = jnp.sum(grad_qkv.astype(jnp.float32), axis=0).reshape(3, local_cols)
    d_b_qv = jnp.stack([grad_cols[0], grad_cols[2]])
    attn_back = contract_cols(grad_qkv, qkv_flat)
    grad_rows = lax.all_to_all(grad_scores, "mp", split_axis=2, concat_axis=1, tiled=True)
    table_part = jnp.transpose(table_grad(grad_rows, rel_pos, rel_x, rel_y))
    input_sum, d_bias_table = (
        lax.psum(attn_back.astype(jnp.bfloat16), "mp").astype(jnp.float32),
        lax.psum(table_part.astype(jnp.bfloat16), "mp").astype(jnp.float32),
    )
    grad_first = grad_one + input_sum
    d_tokens, d_lang_table, d_conv_w, d_conv_b = embed_back(
        grad_first.reshape(page_count, count_of_slots, model_width)
    )
    (
        d_lang_table,
        d_conv_w,
        d_conv_b,
        d_w_qkv,
        d_b_qv,
        d_bias_table,
        d_w_out,
        d_b_out,
        d_ln1_gain,
        d_ln1_bias,
        d_w_in,
        d_b_in,
        d_w_down,
        d_b_down,
        d_ln2_gain,
        d_ln2_bias,
    ) = lax.psum(
        (
            d_lang_table,
            d_conv_w,
            d_conv_b,
            d_w_qkv,
            d_b_qv,
            d_bias_table,
            d_w_out,
            d_b_out,
            d_ln1_gain,
            d_ln1_bias,
            d_w_in,
            d_b_in,
            d_w_down,
            d_b_down,
            d_ln2_gain,
            d_ln2_bias,
        ),
        "dp",
    )
    return (
        result.astype(jnp.bfloat16),
        d_tokens.reshape(total_rows, model_width).astype(jnp.bfloat16),
        d_lang_table,
        d_conv_w,
        d_conv_b,
        d_w_qkv,
        d_b_qv,
        d_bias_table,
        d_w_out,
        d_b_out,
        d_ln1_gain,
        d_ln1_bias,
        d_w_in,
        d_b_in,
        d_w_down,
        d_b_down,
        d_ln2_gain,
        d_ln2_bias,
    )


def solution(mesh):
    in_specs = (
        P("dp", None),
        P("dp"),
        P("dp"),
        P("dp", "mp", None),
        P("dp", "mp", None),
        P("dp", "mp", None),
        P(),
        P(),
        P(),
        P(None, None, "mp"),
        P(None, "mp"),
        P(),
        P("mp", None),
        P(),
        P(),
        P(),
        P(None, "mp"),
        P("mp"),
        P("mp", None),
        P(),
        P(),
        P(),
        P("dp", None),
    )
    out_specs = (
        P("dp", None),
        P("dp", None),
        P(),
        P(),
        P(),
        P(None, None, "mp"),
        P(None, "mp"),
        P(),
        P("mp", None),
        P(),
        P(),
        P(),
        P(None, "mp"),
        P("mp"),
        P("mp", None),
        P(),
        P(),
        P(),
    )
    return jax.shard_map(body, mesh=mesh, in_specs=in_specs, out_specs=out_specs, check_vma=False)
```

profile of v0, /device:TPU:0, one launch (start us, length us, event | category | flops | bytes accessed | tf_op | source)
XLA Modules:
  0.0 1170.5 jit_solution(16028194539182809648)
XLA Ops:
  7.2 153.9 %while.25 = (s32[]{:T(128)}, bf16[22,12,16,704]{3,2,1,0:T(8,128)(2,1)}, s32[22,16,704]{2,1,0:T(8,128)}, s32[22,16,704]{2,1,0:T(8,128)}, s32[22,16,704]{2,1,0:T(8,128)}, /*index=5*/f32[12,160]{1,0:T(8,128)}, s32[]{:T(128)}) while((s32[]{:T(128)}, bf16[22,12,16,704]{3,2,1,0:T(8,128)(2,1)}, s32[22,16,704]{2,1,0:T(8,128)}, ...), condition=%wide.region_1.2_spmd, body=%wide.region_0.1_spmd.sunk | while | flops 268691456 | bytes 2059873 | solution.py:62
  167.7 6.5 all-to-all-start
  187.3 129.8 %all-to-all-done = bf16[2,12,176,704]{3,2,0,1:T(8,128)(2,1)} async-done(((bf16[2,12,176,704]{3,2,0,1:T(8,128)(2,1)}), bf16[2,12,176,704]{3,2,0,1:T(8,128)(2,1)}, u32[]{:S(2)}, u32[]{:S(2)}) %all-to-all-start) | async-done | bytes 5947424 | tf_op jit(solution)/shard_map/all_to_all | solution.py:176
  320.4 6.2 convert_bitcast_fusion
  326.6 10.5 copy.114
  337.1 14.6 %copy.115 = f32[2,3,704,704]{2,3,1,0:T(8,128)} copy(f32[2,3,704,704]{3,2,1,0:T(8,128)} %bitcast.116) | data formatting | bytes 23789568 | tf_op jit(solution)/shard_map/convert_element_type | solution.py:181
  351.7 9.5 add_select_fusion
  361.2 15.6 %fusion.94 = (f32[2,3,704]{2,1,0:T(4,128)S(1)}, f32[2,3,704,704]{2,3,1,0:T(8,128)}) fusion(f32[2,3,704,704]{2,3,1,0:T(8,128)} %add_select_fusion), kind=kOutput, calls=%fused_computation.168 | output fusion | flops 5948095 | bytes 23806464 | tf_op jit(solution)/shard_map/sub | solution.py:183
  376.8 11.9 %fusion.53 = bf16[2,704,3,64]{1,3,2,0:T(8,128)(2,1)S(1)} fusion(f32[2,704,3,64]{1,0,3,2:T(2,128)} %squeeze.24, f32[3,64]{1,0:T(4,128)S(1)} %add.278, f32[2,3,704]{2,1,0:T(4,128)S(1)} %get-tuple-element.305, f32[2,3,704,704]{2,3,1,0:T(8,128)} %add_select_fusion), kind=kOutput, calls=%fused_computation.115 | convolution fusion | flops 390370112 | bytes 13534464 | tf_op jit(solution)/shard_map/phqk,pkhd->pqhd/dot_general | solution.py:186
  392.0 87.5 %all-reduce.16.cloned.1.call-done = bf16[1408,768]{1,0:T(8,128)(2,1)} async-done(((bf16[1408,768]{1,0:T(8,128)(2,1)}), bf16[1408,768]{1,0:T(8,128)(2,1)}) %all-reduce.16.cloned.1.call-update) | async-done | bytes 2162704 | tf_op jit(solution)/shard_map/psum | solution.py:191
  485.1 12.3 %multiply_convert_fusion.1 = (bf16[1408,768]{1,0:T(8,128)(2,1)S(1)}, f32[1408,768]{1,0:T(8,128)}, f32[1408,768]{1,0:T(8,128)}) fusion(f32[768]{0:T(1024)S(1)} %copy-done.50, bf16[1408,768]{1,0:T(8,128)(2,1)S(1)} %fusion.37, bf16[768,768]{1,0:T(8,128)(2,1)S(1)} %copy-done), kind=kOutput, calls=%fused_computation.69 | convolution fusion | flops 1732313088 | bytes 14158848 | tf_op jit(solution)/shard_map/dot_general | solution.py:195
  502.0 87.4 %all-reduce.18.cloned.1.call-done = bf16[1408,768]{1,0:T(8,128)(2,1)} async-done(((bf16[1408,768]{1,0:T(8,128)(2,1)}), bf16[1408,768]{1,0:T(8,128)(2,1)}) %all-reduce.18.cloned.1.call-update) | async-done | bytes 2162704 | tf_op jit(solution)/shard_map/psum | solution.py:199
  608.6 87.5 %all-reduce.20.cloned.1.call-done = bf16[1408,768]{1,0:T(8,128)(2,1)} async-done(((bf16[1408,768]{1,0:T(8,128)(2,1)}), bf16[1408,768]{1,0:T(8,128)(2,1)}) %all-reduce.20.cloned.1.call-update) | async-done | bytes 2162704 | tf_op jit(solution)/shard_map/psum | solution.py:211
  696.1 6.6 multiply_reduce_fusion.1
  702.7 5.7 fusion.85
  712.0 10.9 multiply_reduce_fusion
  725.2 9.0 multiply_convert_fusion
  734.2 18.2 %copy.125 = bf16[2,3,704,704]{3,0,1,2:T(2,128)(2,1)} copy(bf16[2,3,704,704]{2,3,1,0:T(8,128)(2,1)} %multiply_convert_fusion) | data formatting | bytes 11894784 | tf_op jit(solution)/shard_map/convert_element_type | solution.py:226
  752.3 5.3 all-to-all-start.1
  757.6 11.4 fusion.50
  773.4 4.9 fusion.56
  781.7 5.0 reshape.328
  786.7 4.9 convolution_convert_fusion.2
  791.9 5.2 fusion.96
  797.2 6.4 fusion.78
  810.5 159.4 %all-reduce.22.cloned.1.call-done = bf16[1408,768]{1,0:T(8,128)(2,1)} async-done(((bf16[1408,768]{1,0:T(8,128)(2,1)}), bf16[1408,768]{1,0:T(8,128)(2,1)}) %all-reduce.22.cloned.1.call-update) | async-done | bytes 2162704 | tf_op jit(solution)/shard_map/psum | solution.py:243
  977.3 5.8 multiply_reduce_fusion.3
  990.4 13.8 %reshape.330 = bf16[2,12,11,11264]{3,2,1,0:T(8,128)(2,1)} reshape(bf16[2,4,3,176,704]{4,3,2,1,0:T(8,128)(2,1)} %copy.127) | data formatting | bytes 11894784 | tf_op jit(solution)/shard_map/reshape | solution.py:80
  1004.2 10.4 copy.134
  1014.6 107.7 %while.26 = (s32[]{:T(128)}, f32[12,160]{1,0:T(8,128)S(1)}, bf16[22,12,11264]{2,1,0:T(8,128)(2,1)}, s32[22,16,704]{2,1,0:T(8,128)}, s32[22,16,704]{2,1,0:T(8,128...) while((s32[]{:T(128)}, f32[12,160]{1,0:T(8,128)S(1)}, bf16[22,12,11264]{2,1,0:T(8,128)(2,1)}, ...), condition=%wide.region_29.30_spmd.clone, body=%wide.region_28.29_spmd.clone.sunk | while | flops 52291328 | bytes 1051763 | solution.py:92
  1122.4 9.9 psum.156
  1132.2 23.8 %all-reduce.25 = (f32[8,768]{1,0:T(8,128)}, f32[3,768]{1,0:T(4,128)}, f32[768]{0:T(1024)}, f32[2,192]{1,0:T(2,128)}, f32[160,12]{0,1:T(8,128)}, /*index=5*/f32[7...) all-reduce(f32[8,768]{1,0:T(8,128)S(1)} %fusion.73, ...), channel_id=1, replica_groups=mesh['dp'=8,'mp'=4] {'dp'}, use_global_device_ids=true, to_apply=%region_18.19 | all-reduce | flops 16896 | bytes 131328 | tf_op jit(solution)/shard_map/psum | solution.py:267
  (520 shorter events, 359.4 us)
Async XLA Ops:
  7.2 477.9 %copy-start = (bf16[768,768]{1,0:T(8,128)(2,1)S(1)}, bf16[768,768]{1,0:T(8,128)(2,1)}, u32[]{:S(2)}) copy-start(bf16[768,768]{1,0:T(8,128)(2,1)} %param.43) | copy-start | bytes 3538948
  167.7 6.8 copy-start.39
  167.7 6.9 copy-start.45
  167.7 7.0 copy-start.49
  167.7 7.0 copy-start.51
  167.7 7.2 copy-start.9
  167.7 149.5 %all-to-all-start = ((bf16[2,12,176,704]{3,2,0,1:T(8,128)(2,1)}), bf16[2,12,176,704]{3,2,0,1:T(8,128)(2,1)}, u32[]{:S(2)}, u32[]{:S(2)}) async-start(bf16[2,12,176,704]{3,2,0,1:T(8,128)(2,1)} %copy.112), calls=%async_computation | async-start | bytes 12976128 | tf_op jit(solution)/shard_map/all_to_all | solution.py:176
  174.2 305.3 %all-reduce.16.cloned.1.call-start = ((), (), s32[]{:S(2)}) async-start(), calls=%async_computation.2 | async-start | bytes 4325376 | tf_op jit(solution)/shard_map/psum | solution.py:191
  184.6 167.1 %copy-start.12 = (bf16[2,704,3,64]{1,0,3,2:T(2,128)(2,1)}, bf16[2,704,3,64]{1,0,3,2:T(2,128)(2,1)S(1)}, u32[]{:S(2)}) copy-start(bf16[2,704,3,64]{1,0,3,2:T(2,128)(2,1)S(1)} %convert_element_type.168) | copy-start | bytes 1622020
  187.2 164.5 %copy-start.6 = (f32[2,704,3,64]{1,0,3,2:T(2,128)}, f32[2,704,3,64]{1,0,3,2:T(2,128)S(1)}, u32[]{:S(2)}) copy-start(f32[2,704,3,64]{1,0,3,2:T(2,128)S(1)} %squeeze.25) | copy-start | bytes 3244036
  187.3 164.4 %copy-start.29 = (f32[3,64]{1,0:T(4,128)}, f32[3,64]{1,0:T(4,128)S(1)}, u32[]{:S(2)}) copy-start(f32[3,64]{1,0:T(4,128)S(1)} %add.281) | copy-start | bytes 2308
  376.8 13.0 %copy-start.21 = (bf16[192,768]{1,0:T(8,128)(2,1)S(1)}, bf16[192,768]{1,0:T(8,128)(2,1)}, u32[]{:S(2)}) copy-start(bf16[192,768]{1,0:T(8,128)(2,1)} %param.39) | copy-start | bytes 884740
  388.7 90.8 %copy-start.41 = (f32[768]{0:T(1024)S(1)}, f32[768]{0:T(1024)}, u32[]{:S(2)}) copy-start(f32[768]{0:T(1024)} %param.40) | copy-start | bytes 9220
  389.8 93.2 %copy-start.13 = (bf16[1408,192]{0,1:T(8,128)(2,1)}, bf16[1408,192]{0,1:T(8,128)(2,1)S(1)}, u32[]{:S(2)}) copy-start(bf16[1408,192]{0,1:T(8,128)(2,1)S(1)} %reshape.326) | copy-start | bytes 1622020
  391.9 197.5 %all-reduce.18.cloned.1.call-start = ((), (), s32[]{:S(2)}) async-start(), calls=%async_computation.3 | async-start | bytes 4325376 | tf_op jit(solution)/shard_map/psum | solution.py:199
  485.1 13.6 %copy-start.46 = (bf16[768,768]{1,0:T(8,128)(2,1)S(1)}, bf16[768,768]{1,0:T(8,128)(2,1)}, u32[]{:S(2)}) copy-start(bf16[768,768]{1,0:T(8,128)(2,1)} %param.45) | copy-start | bytes 3538948
  498.7 90.7 %copy-start.40 = (f32[768]{0:T(1024)S(1)}, f32[768]{0:T(1024)}, u32[]{:S(2)}) copy-start(f32[768]{0:T(1024)} %param.46) | copy-start | bytes 9220
  501.9 194.1 %all-reduce.20.cloned.1.call-start = ((), (), s32[]{:S(2)}) async-start(), calls=%async_computation.4 | async-start | bytes 4325376 | tf_op jit(solution)/shard_map/psum | solution.py:211
  702.7 7.8 copy-start.22
  712.0 10.9 slice-start
  712.0 12.0 %slice-start.1 = ((s8[12976128]{0:T(1024)(128)(4,1)}), s8[4194304]{0:T(1024)(128)(4,1)S(1)}, s32[]{:S(2)}) async-start(s8[12976128]{0:T(1024)(128)(4,1)} %bitcast.117), calls=%async_computation.8 | async-start | bytes 8388608
  712.0 13.2 %slice-start.2 = ((s8[12976128]{0:T(1024)(128)(4,1)}), s8[4194304]{0:T(1024)(128)(4,1)S(1)}, s32[]{:S(2)}) async-start(s8[12976128]{0:T(1024)(128)(4,1)} %bitcast.117), calls=%async_computation.9 | async-start | bytes 8388608
  712.0 13.2 %slice-start.3 = ((s8[12976128]{0:T(1024)(128)(4,1)}), s8[393216]{0:T(1024)(128)(4,1)S(1)}, s32[]{:S(2)}) async-start(s8[12976128]{0:T(1024)(128)(4,1)} %bitcast.117), calls=%async_computation.10 | async-start | bytes 786432
  752.3 231.1 %all-to-all-start.1 = ((bf16[2,3,704,704]{3,0,1,2:T(2,128)(2,1)}), bf16[2,3,704,704]{3,0,1,2:T(2,128)(2,1)}, u32[]{:S(2)}, u32[]{:S(2)}) async-start(bf16[2,3,704,704]{3,0,1,2:T(2,128)(2,1)} %copy.125), calls=%async_computation.1 | async-start | bytes 12976128 | tf_op jit(solution)/shard_map/all_to_all | solution.py:240
  757.6 212.4 %all-reduce.22.cloned.1.call-start = ((), (), s32[]{:S(2)}) async-start(), calls=%async_computation.5 | async-start | bytes 4325376 | tf_op jit(solution)/shard_map/psum | solution.py:243
  791.6 364.4 %all-reduce.24.cloned.1.call-start = ((), (), s32[]{:S(2)}) async-start(), calls=%async_computation.6 | async-start | bytes 14155776 | tf_op jit(solution)/shard_map/psum | solution.py:267
  810.4 159.5 %copy-start.10 = (bf16[1408,768]{1,0:T(8,128)(2,1)S(1)}, bf16[1408,768]{1,0:T(8,128)(2,1)}, u32[]{:S(2)}) copy-start(bf16[1408,768]{1,0:T(8,128)(2,1)} %param.27) | copy-start | bytes 6488068
  810.4 159.5 %copy-start.28 = (f32[2,768]{1,0:T(2,128)S(1)}, f32[2,768]{1,0:T(2,128)}, u32[]{:S(2)}) copy-start(f32[2,768]{1,0:T(2,128)} %copy-done.27) | copy-start | bytes 18436
  810.5 164.0 %copy-start.32 = (f32[768]{0:T(1024)S(1)}, f32[768]{0:T(1024)}, u32[]{:S(2)}) copy-start(f32[768]{0:T(1024)} %copy-done.31) | copy-start | bytes 9220
  810.5 164.0 %copy-start.34 = (f32[768]{0:T(1024)S(1)}, f32[768]{0:T(1024)}, u32[]{:S(2)}) copy-start(f32[768]{0:T(1024)} %copy-done.33) | copy-start | bytes 9220
  810.5 164.0 %copy-start.36 = (f32[768]{0:T(1024)S(1)}, f32[768]{0:T(1024)}, u32[]{:S(2)}) copy-start(f32[768]{0:T(1024)} %copy-done.35) | copy-start | bytes 9220
  969.9 7.4 slice-start.4
  (40 other events, 125.8 us)
Sparse Core Ops, SparseCore 0:
  392.0 87.3 all-reduce.15
  502.1 87.2 all-reduce.17
  608.7 87.2 all-reduce.19
  791.7 178.1 all-reduce.21
  974.6 111.6 all-reduce.23
where the time goes:
time: 1180 us; the launch traced here: 1170 us
  waiting for transfers between devices  552 us (47%)
  matrix products  256 us (22%)
  local copies, waits for them, and re-layouts  189 us (16%)
  other arithmetic  113 us (10%)
  blocking collectives  33.6 us (3%)
  between operations  14.8 us (1%)
  starting transfers between devices  12.4 us (1%)
    psum x1, waiting for transfers between devices, body(): lax.psum(attn_back.astype(jnp.bfloat16), 'mp').astype(jnp.float32)  159 us
    all_to_all x1, waiting for transfers between devices, body(): lax.all_to_all(row_bias, 'mp', split_axis=1, concat_axis=2, tiled=True)  130 us
    psum x1, waiting for transfers between devices, body(): lax.psum(attn_part.astype(jnp.bfloat16), 'mp').astype(jnp.float32)  87.5 us
    psum x1, waiting for transfers between devices, body(): lax.psum(ffn_back.astype(jnp.bfloat16), 'mp').astype(jnp.float32)  87.5 us
    psum x1, waiting for transfers between devices, body(): ffn_sum = lax.psum(ffn_part.astype(jnp.bfloat16), 'mp').astype(jnp.float32)  87.4 us
    dot_general x22, matrix products, one_block(): looked_up = jnp.dot(table_rows, bucket_hit, precision=lax.Precision.HIGHEST)  86.8 us
    dot_general x26, matrix products, contract_cols(): lax.dot_general(left_side, right_side, (((1,), (1,)), ((), ())), preferre...  78.2 us
    add x44, other arithmetic, bucket_hits(): third_hit = bucket_index == y_ids.reshape(1, -1) + NB1 + NB2  36.8 us
  transfers between devices with their start and end apart: 7, of which 5 were waited for; matrix products, arithmetic and copies ran while one was open for 19% of the time, Pallas kernels for 0%

commit v1 on v0

--- a/solution.py
+++ b/solution.py
@@ -11,6 +11,12 @@
 CONV_DILATION = 2
 norm_eps = 1e-05
 masked_score = -1000000000.0
+
+
+def name_vectors(matrix, comm_axis):
+    res = lax.all_gather(matrix, axis_name=comm_axis)
+    met_up = jnp.sum(res, axis=0)
+    return met_up
 
 
 def layer_norm(inputs, norm_gain, norm_shift):
@@ -240,7 +246,7 @@
     grad_rows = lax.all_to_all(grad_scores, "mp", split_axis=2, concat_axis=1, tiled=True)
     table_part = jnp.transpose(table_grad(grad_rows, rel_pos, rel_x, rel_y))
     input_sum, d_bias_table = (
-        lax.psum(attn_back.astype(jnp.bfloat16), "mp").astype(jnp.float32),
+        name_vectors(attn_back.astype(jnp.bfloat16), comm_axis="mp").astype(jnp.float32),
         lax.psum(table_part.astype(jnp.bfloat16), "mp").astype(jnp.float32),
     )
     grad_first = grad_one + input_sum

time: 1180 us -> 1270 us (1.076)
  waiting for transfers between devices: 552 us -> 642 us
    all_to_all x1, waiting for transfers between devices: 0.01 us -> 249 us  [body(): lax.all_to_all(grad_scores, 'mp', split_axis=2, concat_axis=1, tiled=True)]
    psum x1 -> x0, waiting for transfers between devices: 159 us -> none  [body(): lax.psum(attn_back.astype(jnp.bfloat16), 'mp').astype(jnp.float32)]
    unnamed x135 -> x153, local copies, waits for them, and re-layouts: 26.6 us -> 25.2 us
  transfers between devices with their start and end apart: 7 -> 7, of which waited for: 5 -> 5; matrix products, arithmetic and copies ran while one was open for 19% -> 16% of each run, Pallas kernels for 0% -> 0%
where the time goes in v1:
time: 1270 us; the launch traced here: 1260 us
  waiting for transfers between devices  642 us (51%)
  matrix products  251 us (20%)
  local copies, waits for them, and re-layouts  186 us (15%)
  other arithmetic  118 us (9%)
  blocking collectives  33.4 us (3%)
  between operations  15.2 us (1%)
    all_to_all x1, waiting for transfers between devices, body(): lax.all_to_all(grad_scores, 'mp', split_axis=2, concat_axis=1, tiled=True)  249 us
    all_to_all x1, waiting for transfers between devices, body(): lax.all_to_all(row_bias, 'mp', split_axis=1, concat_axis=2, tiled=True)  130 us
    psum x1, waiting for transfers between devices, body(): lax.psum(attn_part.astype(jnp.bfloat16), 'mp').astype(jnp.float32)  87.5 us
    psum x1, waiting for transfers between devices, body(): lax.psum(ffn_back.astype(jnp.bfloat16), 'mp').astype(jnp.float32)  87.4 us
    psum x1, waiting for transfers between devices, body(): ffn_sum = lax.psum(ffn_part.astype(jnp.bfloat16), 'mp').astype(jnp.float32)  87.4 us
    dot_general x22, matrix products, one_block(): looked_up = jnp.dot(table_rows, bucket_hit, precision=lax.Precision.HIGHEST)  86.8 us
    dot_general x26, matrix products, contract_cols(): lax.dot_general(left_side, right_side, (((1,), (1,)), ((), ())), preferre...  78.6 us
    add x44, other arithmetic, bucket_hits(): third_hit = bucket_index == y_ids.reshape(1, -1) + NB1 + NB2  36.8 us
  transfers between devices with their start and end apart: 7, of which 5 were waited for; matrix products, arithmetic and copies ran while one was open for 16% of the time, Pallas kernels for 0%

profile of v1, /device:TPU:0, one launch (start us, length us, event | category | flops | bytes accessed | tf_op | source)
XLA Modules:
  0.0 1259.4 jit_solution(7807050166041728749)
XLA Ops:
  7.2 153.8 %while.25 = (s32[]{:T(128)}, bf16[22,12,16,704]{3,2,1,0:T(8,128)(2,1)}, s32[22,16,704]{2,1,0:T(8,128)}, s32[22,16,704]{2,1,0:T(8,128)}, s32[22,16,704]{2,1,0:T(8,128)}, /*index=5*/f32[12,160]{1,0:T(8,128)}, s32[]{:T(128)}) while((s32[]{:T(128)}, bf16[22,12,16,704]{3,2,1,0:T(8,128)(2,1)}, s32[22,16,704]{2,1,0:T(8,128)}, ...), condition=%wide.region_1.2_spmd, body=%wide.region_0.1_spmd.sunk | while | flops 268691456 | bytes 2059873 | solution.py:68
  167.5 6.5 all-to-all-start
  187.1 130.0 %all-to-all-done = bf16[2,12,176,704]{3,2,0,1:T(8,128)(2,1)} async-done(((bf16[2,12,176,704]{3,2,0,1:T(8,128)(2,1)}), bf16[2,12,176,704]{3,2,0,1:T(8,128)(2,1)}, u32[]{:S(2)}, u32[]{:S(2)}) %all-to-all-start) | async-done | bytes 5947424 | tf_op jit(solution)/shard_map/all_to_all | solution.py:182
  320.3 6.2 convert_bitcast_fusion
  326.5 10.5 copy.114
  337.0 14.7 %copy.115 = f32[2,3,704,704]{2,3,1,0:T(8,128)} copy(f32[2,3,704,704]{3,2,1,0:T(8,128)} %bitcast.117) | data formatting | bytes 23789568 | tf_op jit(solution)/shard_map/convert_element_type | solution.py:187
  351.7 9.1 add_select_fusion
  360.7 16.2 %fusion.94 = (f32[2,3,704]{2,1,0:T(4,128)}, f32[2,3,704,704]{2,3,1,0:T(8,128)}) fusion(f32[2,3,704,704]{2,3,1,0:T(8,128)} %add_select_fusion), kind=kOutput, calls=%fused_computation.168 | output fusion | flops 5948095 | bytes 23806464 | tf_op jit(solution)/shard_map/sub | solution.py:189
  376.9 11.9 fusion.53
  395.8 87.5 %all-reduce.15.cloned.1.call-done = bf16[1408,768]{1,0:T(8,128)(2,1)} async-done(((bf16[1408,768]{1,0:T(8,128)(2,1)}), bf16[1408,768]{1,0:T(8,128)(2,1)}) %all-reduce.15.cloned.1.call-update) | async-done | bytes 2162704 | tf_op jit(solution)/shard_map/psum | solution.py:197
  488.8 12.3 multiply_convert_fusion.1
  505.8 87.4 %all-reduce.17.cloned.1.call-done = bf16[1408,768]{1,0:T(8,128)(2,1)} async-done(((bf16[1408,768]{1,0:T(8,128)(2,1)}), bf16[1408,768]{1,0:T(8,128)(2,1)}) %all-reduce.17.cloned.1.call-update) | async-done | bytes 2162704 | tf_op jit(solution)/shard_map/psum | solution.py:205
  613.7 87.4 %all-reduce.19.cloned.1.call-done = bf16[1408,768]{1,0:T(8,128)(2,1)} async-done(((bf16[1408,768]{1,0:T(8,128)(2,1)}), bf16[1408,768]{1,0:T(8,128)(2,1)}) %all-reduce.19.cloned.1.call-update) | async-done | bytes 2162704 | tf_op jit(solution)/shard_map/psum | solution.py:217
  701.1 7.2 multiply_reduce_fusion.1
  708.3 5.7 fusion.85
  717.5 11.3 fusion.50
  728.8 11.8 multiply_reduce_fusion
  741.7 6.1 multiply_convert_fusion
  755.7 4.7 convolution_convert_fusion.2
  760.4 18.4 %copy.125 = bf16[2,3,704,704]{3,0,1,2:T(2,128)(2,1)} copy(bf16[2,3,704,704]{2,3,1,0:T(8,128)(2,1)} %copy-done.3) | data formatting | bytes 11894784 | tf_op jit(solution)/shard_map/convert_element_type | solution.py:232
  778.8 5.4 all-to-all-start.1
  784.5 5.2 fusion.96
  789.8 6.0 fusion.78
  802.7 249.2 %all-to-all-done.1 = bf16[2,3,704,704]{3,0,1,2:T(2,128)(2,1)} async-done(((bf16[2,3,704,704]{3,0,1,2:T(2,128)(2,1)}), bf16[2,3,704,704]{3,0,1,2:T(2,128)(2,1)}, u32[]{:S(2)}, u32[]{:S(2)}) %all-to-all-start.1) | async-done | bytes 5947424 | tf_op jit(solution)/shard_map/all_to_all | solution.py:246
  1059.0 14.0 %reshape.330 = bf16[2,12,11,11264]{3,2,1,0:T(8,128)(2,1)} reshape(bf16[2,4,3,176,704]{4,3,2,1,0:T(8,128)(2,1)} %copy.127) | data formatting | bytes 11894784 | tf_op jit(solution)/shard_map/reshape | solution.py:86
  1073.0 10.4 copy.134
  1083.4 107.6 %while.26 = (s32[]{:T(128)}, f32[12,160]{1,0:T(8,128)S(1)}, bf16[22,12,11264]{2,1,0:T(8,128)(2,1)}, s32[22,16,704]{2,1,0:T(8,128)}, s32[22,16,704]{2,1,0:T(8,128...) while((s32[]{:T(128)}, f32[12,160]{1,0:T(8,128)S(1)}, bf16[22,12,11264]{2,1,0:T(8,128)(2,1)}, ...), condition=%wide.region_29.30_spmd.clone, body=%wide.region_28.29_spmd.clone.sunk | while | flops 52291328 | bytes 1051763 | solution.py:98
  1191.0 9.4 psum.148
  1200.4 6.8 reduce_sum.232
  1207.3 4.5 fusion.82
  1214.7 5.5 multiply_reduce_fusion.3
  1220.6 24.0 %all-reduce.22 = (f32[8,768]{1,0:T(8,128)}, f32[3,768]{1,0:T(4,128)}, f32[768]{0:T(1024)}, f32[2,192]{1,0:T(2,128)}, f32[160,12]{0,1:T(8,128)}, /*index=5*/f32[7...) all-reduce(f32[8,768]{1,0:T(8,128)S(1)} %fusion.73, ...), channel_id=1, replica_groups=mesh['dp'=8,'mp'=4] {'dp'}, use_global_device_ids=true, to_apply=%region_18.19 | all-reduce | flops 16896 | bytes 131328 | tf_op jit(solution)/shard_map/psum | solution.py:273
  (539 shorter events, 358.5 us)
Async XLA Ops:
  7.2 481.6 %copy-start = (bf16[768,768]{1,0:T(8,128)(2,1)S(1)}, bf16[768,768]{1,0:T(8,128)(2,1)}, u32[]{:S(2)}) copy-start(bf16[768,768]{1,0:T(8,128)(2,1)} %param.43) | copy-start | bytes 3538948
  167.5 7.0 copy-start.45
  167.5 7.0 copy-start.53
  167.5 7.2 copy-start.58
  167.5 7.2 copy-start.60
  167.5 7.4 copy-start.10
  167.5 149.5 %all-to-all-start = ((bf16[2,12,176,704]{3,2,0,1:T(8,128)(2,1)}), bf16[2,12,176,704]{3,2,0,1:T(8,128)(2,1)}, u32[]{:S(2)}, u32[]{:S(2)}) async-start(bf16[2,12,176,704]{3,2,0,1:T(8,128)(2,1)} %copy.112), calls=%async_computation | async-start | bytes 12976128 | tf_op jit(solution)/shard_map/all_to_all | solution.py:182
  174.0 309.2 %all-reduce.15.cloned.1.call-start = ((), (), s32[]{:S(2)}) async-start(), calls=%async_computation.2 | async-start | bytes 4325376 | tf_op jit(solution)/shard_map/psum | solution.py:197
  184.0 192.9 %copy-start.51 = (f32[3,64]{1,0:T(4,128)}, f32[3,64]{1,0:T(4,128)S(1)}, u32[]{:S(2)}) copy-start(f32[3,64]{1,0:T(4,128)S(1)} %add.276) | copy-start | bytes 2308
  187.1 164.6 %copy-start.30 = (f32[3,64]{1,0:T(4,128)}, f32[3,64]{1,0:T(4,128)S(1)}, u32[]{:S(2)}) copy-start(f32[3,64]{1,0:T(4,128)S(1)} %add.279) | copy-start | bytes 2308
  388.8 94.4 %copy-start.47 = (f32[768]{0:T(1024)S(1)}, f32[768]{0:T(1024)}, u32[]{:S(2)}) copy-start(f32[768]{0:T(1024)} %param.40) | copy-start | bytes 9220
  392.4 94.4 %copy-start.13 = (bf16[1408,192]{0,1:T(8,128)(2,1)}, bf16[1408,192]{0,1:T(8,128)(2,1)S(1)}, u32[]{:S(2)}) copy-start(bf16[1408,192]{0,1:T(8,128)(2,1)S(1)} %reshape.326) | copy-start | bytes 1622020
  395.7 197.5 %all-reduce.17.cloned.1.call-start = ((), (), s32[]{:S(2)}) async-start(), calls=%async_computation.3 | async-start | bytes 4325376 | tf_op jit(solution)/shard_map/psum | solution.py:205
  488.8 12.4 copy-start.7
  488.8 13.7 %copy-start.54 = (bf16[768,768]{1,0:T(8,128)(2,1)S(1)}, bf16[768,768]{1,0:T(8,128)(2,1)}, u32[]{:S(2)}) copy-start(bf16[768,768]{1,0:T(8,128)(2,1)} %param.45) | copy-start | bytes 3538948
  502.5 90.7 %copy-start.46 = (f32[768]{0:T(1024)S(1)}, f32[768]{0:T(1024)}, u32[]{:S(2)}) copy-start(f32[768]{0:T(1024)} %param.46) | copy-start | bytes 9220
  505.7 195.3 %all-reduce.19.cloned.1.call-start = ((), (), s32[]{:S(2)}) async-start(), calls=%async_computation.4 | async-start | bytes 4325376 | tf_op jit(solution)/shard_map/psum | solution.py:217
  613.6 586.8 %all-gather.3.cloned.1.call-start = ((), (), s32[]{:S(2)}) async-start(), calls=%async_computation.5 | async-start | bytes 10813440 | tf_op jit(solution)/shard_map/all_gather | solution.py:17
  701.1 7.2 copy-start.12
  708.3 7.7 copy-start.21
  717.5 11.3 copy-start.22
  728.8 11.8 slice-start
  728.8 11.8 slice-start.1
  728.8 12.9 %slice-start.2 = ((s8[12976128]{0:T(1024)(128)(4,1)}), s8[4194304]{0:T(1024)(128)(4,1)S(1)}, s32[]{:S(2)}) async-start(s8[12976128]{0:T(1024)(128)(4,1)} %bitcast.118), calls=%async_computation.9 | async-start | bytes 8388608
  728.8 12.9 %slice-start.3 = ((s8[12976128]{0:T(1024)(128)(4,1)}), s8[393216]{0:T(1024)(128)(4,1)S(1)}, s32[]{:S(2)}) async-start(s8[12976128]{0:T(1024)(128)(4,1)} %bitcast.118), calls=%async_computation.10 | async-start | bytes 786432
  728.8 12.9 %copy-start.26 = (f32[2,3,704]{2,1,0:T(4,128)S(1)}, f32[2,3,704]{2,1,0:T(4,128)}, u32[]{:S(2)}) copy-start(f32[2,3,704]{2,1,0:T(4,128)} %get-tuple-element.305) | copy-start | bytes 50692
  778.8 273.1 %all-to-all-start.1 = ((bf16[2,3,704,704]{3,0,1,2:T(2,128)(2,1)}), bf16[2,3,704,704]{3,0,1,2:T(2,128)(2,1)}, u32[]{:S(2)}, u32[]{:S(2)}) async-start(bf16[2,3,704,704]{3,0,1,2:T(2,128)(2,1)} %copy.125), calls=%async_computation.1 | async-start | bytes 12976128 | tf_op jit(solution)/shard_map/all_to_all | solution.py:246
  784.2 460.5 %all-reduce.21.cloned.1.call-start = ((), (), s32[]{:S(2)}) async-start(), calls=%async_computation.6 | async-start | bytes 14155776 | tf_op jit(solution)/shard_map/psum | solution.py:273
  1200.4 6.8 copy-start.11
  1200.4 6.8 copy-start.29
  1207.3 7.4 slice-start.4
  1244.7 6.4 copy-start.15
  (49 other events, 171.1 us)
Sparse Core Ops, SparseCore 0:
  395.8 87.3 all-reduce.14
  505.9 87.2 all-reduce.16
  613.7 87.2 all-reduce.18
  760.5 285.5 all-gather.2
  1050.7 110.7 all-reduce.20
